TPU v7x, 32 devices: a whole 2x2x4 slice. The times are simulated.
32 devices in a mesh: blk: 32 (over z, y, x, core), feat: 1.
Axes of the slice: x: 2, y: 2, z: 4, core: 2. Of those that a mesh axis runs over, the one named last changes fastest.
Arguments:
- activations: bfloat16 [5120, 4096], P('blk', 'feat'), may hold values from -6 to 6
- live_rows: int32 [32], replicated, may hold values from 1 to 160, as said below
- encoder_weight: bfloat16 [4096, 32768], P('feat', 'blk'), may hold values from -0.09375 to 0.09375
- encoder_bias: float32 [32768], P('blk'), may hold values from -3 to 3
- decoder_weight: bfloat16 [4, 1024, 32768], P(None, 'feat', 'blk'), may hold values from -0.09375 to 0.09375
- decoder_bias: float32 [32768], P('blk'), may hold values from -3 to 3
- targets: bfloat16 [640, 32768], P('feat', 'blk'), may hold values from -6 to 6
Outputs:
- reconstruction: float32 [640, 32768], P('feat', 'blk')
- decoder_grad: float32 [4, 1024, 32768], P(None, 'feat', 'blk')
Inputs may be any that keep to these rules, and one draw needn't show every extreme that they name: `live_rows`: live rows of a block of 160 slots are its first ones; some block is full.
All inputs are finite; a program needn't handle non-finite values.
Results may differ from a plain program's by a relative error of at most 0.015.
Values may be sent and summed in bfloat16 or wider, within the bound.
A program may use at most 128 MiB of HBM per device.

v0:
```python
import functools

import jax
import jax.numpy as jnp
from jax import lax
from jax.experimental import pallas as pl
from jax.experimental.pallas import tpu as pltpu
from jax.sharding import PartitionSpec as P

G = 8
MESH = pl.DeviceIdType.MESH


def gather_kernel(
    pieces,
    act_hbm,
    live_ref,
    enc_hbm,
    bias_ref,
    dec_hbm,
    codes_hbm,
    summed_hbm,
    acts,
    enc,
    dec,
    codes,
    part,
    summed,
    load_sem,
    s1_send,
    s1_recv,
    s2_send,
    s2_recv,
    s3_send,
    s3_recv,
    t1_send,
    t1_recv,
    t2_send,
    t2_recv,
    t3_send,
    t3_recv,
    out_sem,
):
    position = lax.axis_index("blk")
    share = lax.axis_index("feat")
    base = position // 4 * 4
    me = position % 4
    core = me % 2
    home = me - core
    away = 2 - home
    twin = home + 1 - core
    peer = away + core
    peer_twin = away + 1 - core
    on_chip = (base + twin, share)
    across = (base + peer, share)

    rows = acts.shape[1]
    piece = rows // pieces
    width = enc.shape[1]
    tile = min(256, width)
    tiles = width // tile

    def at_piece(h):
        return pl.ds(h * piece, piece)

    load_act = pltpu.make_async_copy(act_hbm, acts.at[me], load_sem.at[0])
    load_enc = pltpu.make_async_copy(enc_hbm, enc, load_sem.at[1])
    load_dec = pltpu.make_async_copy(dec_hbm, dec, load_sem.at[2])
    load_act.start()
    load_enc.start()
    load_dec.start()

    barrier = pltpu.get_barrier_semaphore()
    for neighbour in (on_chip, across):
        pl.semaphore_signal(barrier, inc=1, device_id=neighbour, device_id_type=MESH)
    pl.semaphore_wait(barrier, 2)

    def remote(src, dst, send, recv, to):
        return pltpu.make_async_remote_copy(
            src_ref=src,
            dst_ref=dst,
            send_sem=send,
            recv_sem=recv,
            device_id=to,
            device_id_type=MESH,
        )

    def s1(b):
        return remote(act_hbm, acts.at[b], s1_send.at[0], s1_recv.at[0], on_chip)

    def s2(b, h):
        return remote(
            act_hbm.at[at_piece(h)],
            acts.at[b, at_piece(h)],
            s2_send.at[h],
            s2_recv.at[h],
            across,
        )

    def s3(b, h):
        ref = acts.at[b, at_piece(h)]
        return remote(ref, ref, s3_send.at[h], s3_recv.at[h], on_chip)

    def t1(f, b):
        ref = codes.at[f, b]
        return remote(ref, ref, t1_send.at[b], t1_recv.at[b], on_chip)

    def t2(f, b, h):
        ref = codes.at[f, b, at_piece(h)]
        return remote(ref, ref, t2_send.at[b, h], t2_recv.at[b, h], across)

    def t3(f, b, h):
        ref = codes.at[f, b, at_piece(h)]
        return remote(ref, ref, t3_send.at[b, h], t3_recv.at[b, h], on_chip)

    for h in range(pieces):
        s2(me, h).start()
    s1(me).start()

    def encode(b):
        live = live_ref[base + b]
        keep = lax.broadcasted_iota(jnp.int32, (rows, tile), 0) < live

        def column(n, carry):
            at = pl.ds(pl.multiple_of(n * tile, tile), tile)
            product = jnp.dot(acts[b], enc[:, at], preferred_element_type=jnp.float32)
            value = product.astype(jnp.bfloat16).astype(jnp.float32) + bias_ref[:, at]
            value = jnp.where(keep, jnp.maximum(value, 0.0), 0.0)
            codes[me, b, :, at] = value.astype(jnp.bfloat16)
            return carry

        lax.fori_loop(0, tiles, column, 0)

    def product_of(fs, b, at, h=None):
        total = None
        for f in fs:
            left = codes[f, b] if h is None else codes[f, b, at_piece(h)]
            term = jnp.dot(left, dec[f, :, at], preferred_element_type=jnp.float32)
            total = term if total is None else total + term
        return total

    def out_codes(b, h):
        return pltpu.make_async_copy(
            codes.at[:, b, at_piece(h)], codes_hbm.at[:, b, at_piece(h)], out_sem.at[0, b, h]
        )

    def out_summed(b, h):
        return pltpu.make_async_copy(
            summed.at[b, at_piece(h)], summed_hbm.at[b, at_piece(h)], out_sem.at[1, b, h]
        )

    load_act.wait()
    load_enc.wait()
    encode(me)
    s1(twin).wait_recv()
    t1(me, me).start()
    encode(twin)
    t1(me, twin).start()
    for b in (home, home + 1):
        for h in range(pieces):
            t2(me, b, h).start()
    t1(twin, home).wait_recv()
    t1(twin, home + 1).wait_recv()
    load_dec.wait()

    def half(b, slot):
        def column(n, carry):
            at = pl.ds(pl.multiple_of(n * tile, tile), tile)
            part[slot, :, at] = product_of((home, home + 1), b, at)
            return carry

        lax.fori_loop(0, tiles, column, 0)

    def half_step(slot, carry):
        half(home + slot, slot)
        return carry

    lax.fori_loop(0, 2, half_step, 0)

    for h in range(pieces):
        s2(peer, h).wait_recv()
        s3(peer, h).start()
    encode(peer)
    t1(me, peer).start()
    for h in range(pieces):
        s3(peer_twin, h).wait_recv()
    encode(peer_twin)
    t1(me, peer_twin).start()
    for b in (away, away + 1):
        for h in range(pieces):
            t2(me, b, h).start()
    for b in (away, away + 1):
        for h in range(pieces):
            t2(peer, b, h).wait_recv()
            t3(peer, b, h).start()
    t1(twin, away).wait_recv()
    t1(twin, away + 1).wait_recv()

    def away_step(i, carry):
        b = away + i
        for h in range(pieces):
            t3(peer_twin, b, h).wait_recv()
            out_codes(b, h).start()

        def column(n, inner):
            at = pl.ds(pl.multiple_of(n * tile, tile), tile)
            summed[b, :, at] = product_of((0, 1, 2, 3), b, at).astype(jnp.bfloat16)
            return inner

        lax.fori_loop(0, tiles, column, 0)
        for h in range(pieces):
            out_summed(b, h).start()
        return carry

    lax.fori_loop(0, 2, away_step, 0)

    def home_step(i, carry):
        b = home + i
        for h in range(pieces):
            t2(peer, b, h).wait_recv()
            t3(peer, b, h).start()
            t3(peer_twin, b, h).wait_recv()
            out_codes(b, h).start()

            def column(n, inner):
                at = pl.ds(pl.multiple_of(n * tile, tile), tile)
                total = part[i, at_piece(h), at] + product_of((away, away + 1), b, at, h)
                summed[b, at_piece(h), at] = total.astype(jnp.bfloat16)
                return inner

            lax.fori_loop(0, tiles, column, 0)
            out_summed(b, h).start()
        return carry

    lax.fori_loop(0, 2, home_step, 0)

    s1(me).wait_send()
    for h in range(pieces):
        s2(me, h).wait_send()
        s3(peer, h).wait_send()
    for b in range(4):
        t1(me, b).wait_send()
        for h in range(pieces):
            t2(me, b, h).wait_send()
            t3(peer, b, h).wait_send()
            out_codes(b, h).wait()
            out_summed(b, h).wait()


def gradient_kernel(
    live_ref, codes_ref, summed_ref, bias_ref, targets_ref, grad_ref, rebuilt_hbm, residual, rebuilt, sem
):
    step = pl.program_id(0)
    copy = pltpu.make_async_copy(rebuilt, rebuilt_hbm, sem)

    @pl.when(step == 0)
    def _():
        base = lax.axis_index("blk") // 4 * 4
        rows, width = summed_ref.shape[1:]
        for b in range(4):
            at = pl.ds(b * rows, rows)
            whole = summed_ref[b].astype(jnp.float32) + bias_ref[...]
            rebuilt[at, :] = whole
            keep = lax.broadcasted_iota(jnp.int32, (rows, width), 0) < live_ref[base + b]
            error = jnp.where(keep, whole - targets_ref[at, :].astype(jnp.float32), 0.0)
            residual[at, :] = error.astype(jnp.bfloat16)
        copy.start()

    grad_ref[0] = lax.dot_general(
        codes_ref[0], residual[...], (((0,), (0,)), ((), ())), preferred_element_type=jnp.float32
    )

    @pl.when(step == pl.num_programs(0) - 1)
    def _():
        copy.wait()


def four_owners(
    activations, live_rows, encoder_weight, encoder_bias, decoder_weight, decoder_bias, targets
):
    rows, depth = activations.shape
    features = encoder_weight.shape[1]
    width = decoder_weight.shape[2]
    tokens = targets.shape[0]
    pieces = 2 if rows % 32 == 0 else 1
    any_space = pl.BlockSpec(memory_space=pl.ANY)
    in_vmem = pl.BlockSpec(memory_space=pltpu.VMEM)
    in_smem = pl.BlockSpec(memory_space=pltpu.SMEM)
    dma = pltpu.SemaphoreType.DMA
    bf16 = jnp.bfloat16
    codes, summed = pl.pallas_call(
        functools.partial(gather_kernel, pieces),
        out_shape=(
            jax.ShapeDtypeStruct((4, 4, rows, features), bf16),
            jax.ShapeDtypeStruct((4, rows, width), bf16),
        ),
        in_specs=[any_space, in_smem, any_space, in_vmem, any_space],
        out_specs=(any_space, any_space),
        scratch_shapes=[
            pltpu.VMEM((4, rows, depth), bf16),
            pltpu.VMEM((depth, features), bf16),
            pltpu.VMEM((4, features, width), bf16),
            pltpu.VMEM((4, 4, rows, features), bf16),
            pltpu.VMEM((2, rows, width), jnp.float32),
            pltpu.VMEM((4, rows, width), bf16),
            dma((3,)),
            dma((1,)),
            dma((1,)),
            dma((pieces,)),
            dma((pieces,)),
            dma((pieces,)),
            dma((pieces,)),
            dma((4,)),
            dma((4,)),
            dma((4, pieces)),
            dma((4, pieces)),
            dma((4, pieces)),
            dma((4, pieces)),
            dma((2, 4, pieces)),
        ],
        compiler_params=pltpu.CompilerParams(
            collective_id=0, has_side_effects=True, vmem_limit_bytes=60 * 1024 * 1024
        ),
        name="gather_codes",
    )(activations, live_rows, encoder_weight, encoder_bias[None, :], decoder_weight)

    span = min(512, features)
    per = features // span
    grad, rebuilt = pl.pallas_call(
        gradient_kernel,
        grid=(4 * per,),
        out_shape=(
            jax.ShapeDtypeStruct((4, features, width), jnp.float32),
            jax.ShapeDtypeStruct((tokens, width), jnp.float32),
        ),
        in_specs=[
            in_smem,
            pl.BlockSpec((1, tokens, span), lambda i: (i // per, 0, i % per)),
            in_vmem,
            in_vmem,
            in_vmem,
        ],
        out_specs=(pl.BlockSpec((1, span, width), lambda i: (i // per, i % per, 0)), any_space),
        scratch_shapes=[
            pltpu.VMEM((tokens, width), bf16),
            pltpu.VMEM((tokens, width), jnp.float32),
            dma(()),
        ],
        compiler_params=pltpu.CompilerParams(
            dimension_semantics=("arbitrary",), vmem_limit_bytes=60 * 1024 * 1024
        ),
        name="gradient",
    )(live_rows, codes.reshape(4, tokens, features), summed, decoder_bias[None, :], targets)
    return rebuilt, grad


def from_partner(shard, axis, distance):
    return lax.ppermute(shard, axis, [(i, i ^ 1 << distance) for i in range(lax.axis_size(axis))])


def group_rows(block, levels, position):
    for bit in range(levels):
        other = from_partner(block, "blk", bit)
        upper = position >> bit & 1 == 1
        block = jnp.where(
            upper, jnp.concatenate([other, block], 0), jnp.concatenate([block, other], 0)
        )
    return block


def general(
    activations, live_rows, encoder_weight, encoder_bias, decoder_weight, decoder_bias, targets
):
    owners = lax.axis_size("blk") // G
    levels = owners.bit_length() - 1
    shares = lax.axis_size("feat")
    position = lax.axis_index("blk")
    share_index = lax.axis_index("feat")
    group_index = position // owners
    tok_rows = activations.shape[0]
    counts = lax.dynamic_slice_in_dim(live_rows, group_index * owners, owners)
    positions = jnp.arange(tok_rows, dtype=jnp.int32)
    live_mask = (positions[None, :] < counts[:, None]).astype(jnp.float32).reshape(-1)
    gathered = group_rows(activations, levels, position)
    per_share = encoder_weight.shape[1] // shares
    bias_share = lax.dynamic_slice_in_dim(encoder_bias, share_index * per_share, per_share)
    columns = encoder_weight
    whole = lax.psum(
        lax.dot_general(
            columns, gathered, (((0,), (1,)), ((), ())), preferred_element_type=jnp.float32
        ).astype(jnp.bfloat16),
        "feat",
    ).astype(jnp.float32)
    preact = lax.dynamic_slice_in_dim(whole, share_index * per_share, per_share, 0)
    codes_by_feature = (jax.nn.relu(preact + bias_share[:, None]) * live_mask[None, :]).astype(
        jnp.bfloat16
    )
    codes_all = group_rows(codes_by_feature, levels, position)
    decoder_rows = decoder_weight.reshape(-1, decoder_weight.shape[2])
    block_rows = gathered.shape[0] // shares
    columns = codes_all
    summed = lax.psum_scatter(
        lax.dot_general(
            columns, decoder_rows, (((0,), (0,)), ((), ())), preferred_element_type=jnp.float32
        ).astype(jnp.bfloat16),
        "feat",
        scatter_dimension=0,
        tiled=True,
    ).astype(jnp.float32)
    rebuilt = summed + decoder_bias[None, :]
    mask_block = lax.dynamic_slice_in_dim(live_mask, share_index * block_rows, block_rows)
    residual = ((rebuilt - targets.astype(jnp.float32)) * mask_block[:, None]).astype(jnp.bfloat16)
    columns = codes_all
    gradient = jnp.dot(
        columns,
        lax.all_gather(residual, "feat", axis=0, tiled=True),
        preferred_element_type=jnp.float32,
    )
    return (rebuilt, gradient.reshape(decoder_weight.shape))


def solution(mesh):
    in_specs = (
        P("blk", "feat"),
        P(),
        P("feat", "blk"),
        P("blk"),
        P(None, "feat", "blk"),
        P("blk"),
        P("feat", "blk"),
    )
    out_specs = (P("feat", "blk"), P(None, "feat", "blk"))
    fused = mesh.shape["blk"] // G == 4 and mesh.shape["feat"] == 1
    return jax.shard_map(
        four_owners if fused else general,
        mesh=mesh,
        in_specs=in_specs,
        out_specs=out_specs,
        check_vma=False,
    )
```

profile of v0, /device:TPU:0, one launch (start us, length us, event | category | flops | bytes accessed | tf_op | source)
XLA Modules:
  0.0 79.5 jit_solution(12320552409794322922)
XLA Ops:
  0.6 64.8 %gather_codes.1 = (bf16[4,4,160,1024]{3,2,1,0:T(8,128)(2,1)}, bf16[4,160,1024]{2,1,0:T(8,128)(2,1)}) custom-call(bf16[160,4096]{1,0:T(8,128)(2,1)} %act_hbm.1, s32[32]{0:T(128)} %live_ref.3, bf16[4096,1024]{1,0:T(8,128)(2,1)} %enc_hbm.1, f32[1,1024]{1,0:T(1,128)} %bitcast.5, bf16[4,1024,1024]{2,1,0:T(8,128)(2,1)} %dec_hbm.1), custom_call_target="tpu_custom_call" | custom-call | tf_op jit(solution)/shard_map/gather_codes/pallas_call | solution.py:291
  65.4 14.1 %gradient.1 = (f32[4,1024,1024]{2,1,0:T(8,128)}, f32[640,1024]{1,0:T(8,128)}) custom-call(s32[32]{0:T(128)} %live_ref.3, bf16[4,640,1024]{2,1,0:T(8,128)(2,1)} %bitcast.3, bf16[4,160,1024]{2,1,0:T(8,128)(2,1)} %get-tuple-element.7.summed_ref, f32[1,1024]{1,0:T(1,128)} %bitcast.4, bf16[640,1024]{1,0:T(8,128)(2,1)} %targets_ref.1), custom_call_target="tpu_custom_call" | custom-call | tf_op jit(solution)/shard_map/gradient/pallas_call | solution.py:329
where the time goes:
time: 80.1 us; the launch traced here: 79.5 us
  Pallas kernels  78.9 us (99%)
    pallas_call x1, Pallas kernels, four_owners(): pl.pallas_call(functools.partial(gather_kernel, pieces), out_shape=(jax.S...  64.8 us
    pallas_call x1, Pallas kernels, four_owners(): pl.pallas_call(gradient_kernel, grid=(4 * per,), out_shape=(jax.ShapeDtyp...  14.1 us

commit v1 on v0

v1 whole, which is shorter than its diff:
```python
import functools

import jax
import jax.numpy as jnp
from jax import lax
from jax.experimental import pallas as pl
from jax.experimental.pallas import tpu as pltpu
from jax.sharding import PartitionSpec as P

G = 8
MESH = pl.DeviceIdType.MESH


def cuts(rows, parts):
    if rows % 16 or rows // 16 < len(parts):
        return [(0, rows)]
    tiles, total, edges = rows // 16, sum(parts), [0]
    for k in range(1, len(parts)):
        edges.append(max(edges[-1] + 1, tiles * sum(parts[:k]) // total))
    edges.append(tiles)
    return [(16 * a, 16 * (b - a)) for a, b in zip(edges[:-1], edges[1:])]


def gather_kernel(
    act_cuts,
    code_cuts,
    act_hbm,
    live_hbm,
    enc_hbm,
    bias_hbm,
    dec_hbm,
    dec_bias_hbm,
    targets_hbm,
    codes,
    residual,
    rebuilt,
    acts,
    enc,
    dec,
    part,
    targets,
    live_ref,
    bias_ref,
    dec_bias_ref,
    load_sem,
    s1_send,
    s1_recv,
    s2_send,
    s2_recv,
    s3_send,
    s3_recv,
    t1_send,
    t1_recv,
    t2_send,
    t2_recv,
    t3_send,
    t3_recv,
):
    position = lax.axis_index("blk")
    share = lax.axis_index("feat")
    base = position // 4 * 4
    me = position % 4
    core = me % 2
    home = me - core
    away = 2 - home
    twin = home + 1 - core
    peer = away + core
    peer_twin = away + 1 - core
    on_chip = (base + twin, share)
    across = (base + peer, share)

    rows = acts.shape[1]
    width = enc.shape[1]
    tile = min(256, width)
    tiles = width // tile

    load_act = pltpu.make_async_copy(act_hbm, acts.at[me], load_sem.at[0])
    load_enc = pltpu.make_async_copy(enc_hbm, enc, load_sem.at[1])
    load_dec = pltpu.make_async_copy(dec_hbm, dec, load_sem.at[2])
    load_targets = pltpu.make_async_copy(targets_hbm, targets, load_sem.at[3])
    load_live = pltpu.make_async_copy(live_hbm, live_ref, load_sem.at[4])
    load_bias = pltpu.make_async_copy(bias_hbm, bias_ref, load_sem.at[5])
    load_dec_bias = pltpu.make_async_copy(dec_bias_hbm, dec_bias_ref, load_sem.at[6])
    load_live.start()
    load_bias.start()
    load_act.start()
    load_enc.start()
    load_dec_bias.start()

    barrier = pltpu.get_barrier_semaphore()
    for neighbour in (on_chip, across):
        pl.semaphore_signal(barrier, inc=1, device_id=neighbour, device_id_type=MESH)
    pl.semaphore_wait(barrier, 2)

    def remote(src, dst, send, recv, to):
        return pltpu.make_async_remote_copy(
            src_ref=src,
            dst_ref=dst,
            send_sem=send,
            recv_sem=recv,
            device_id=to,
            device_id_type=MESH,
        )

    def s1(b):
        return remote(act_hbm, acts.at[b], s1_send.at[0], s1_recv.at[0], on_chip)

    def s2(b, h):
        at = pl.ds(*act_cuts[h])
        return remote(act_hbm.at[at], acts.at[b, at], s2_send.at[h], s2_recv.at[h], across)

    def s3(b, h):
        ref = acts.at[b, pl.ds(*act_cuts[h])]
        return remote(ref, ref, s3_send.at[h], s3_recv.at[h], on_chip)

    def at_rows(b, start, count):
        return pl.ds(pl.multiple_of(b * rows + start, count if rows % 16 else 16), count)

    def t1(f, b):
        ref = codes.at[f, at_rows(b, 0, rows)]
        return remote(ref, ref, t1_send.at[b], t1_recv.at[b], on_chip)

    def t2(f, b, h):
        ref = codes.at[f, at_rows(b, *code_cuts[h])]
        return remote(ref, ref, t2_send.at[b, h], t2_recv.at[b, h], across)

    def t3(f, b, h):
        ref = codes.at[f, at_rows(b, *code_cuts[h])]
        return remote(ref, ref, t3_send.at[b, h], t3_recv.at[b, h], on_chip)

    every = range(len(code_cuts))
    for h in range(len(act_cuts)):
        s2(me, h).start()
    s1(me).start()
    load_dec.start()
    load_targets.start()

    def encode(b):
        live = live_ref[base + b]
        keep = lax.broadcasted_iota(jnp.int32, (rows, tile), 0) < live

        def column(n, carry):
            at = pl.ds(pl.multiple_of(n * tile, tile), tile)
            product = jnp.dot(acts[b], enc[:, at], preferred_element_type=jnp.float32)
            value = product.astype(jnp.bfloat16).astype(jnp.float32) + bias_ref[:, at]
            value = jnp.where(keep, jnp.maximum(value, 0.0), 0.0)
            codes[me, at_rows(b, 0, rows), at] = value.astype(jnp.bfloat16)
            return carry

        lax.fori_loop(0, tiles, column, 0)

    def home_features(b):
        here = at_rows(b, 0, rows)

        def column(n, carry):
            at = pl.ds(pl.multiple_of(n * tile, tile), tile)
            first = jnp.dot(
                codes[me, here], dec[me, :, at], preferred_element_type=jnp.float32
            )
            second = jnp.dot(
                codes[twin, here], dec[twin, :, at], preferred_element_type=jnp.float32
            )
            part[here, at] = first + second
            return carry

        lax.fori_loop(0, tiles, column, 0)

    def finish(b, h):
        start, count = code_cuts[h]
        here = at_rows(b, start, count)
        t2(peer, b, h).wait_recv()
        t3(peer, b, h).start()
        part[here] += jnp.dot(codes[peer, here], dec[peer], preferred_element_type=jnp.float32)
        t3(peer_twin, b, h).wait_recv()
        whole = part[here] + jnp.dot(
            codes[peer_twin, here], dec[peer_twin], preferred_element_type=jnp.float32
        )
        whole = whole.astype(jnp.bfloat16).astype(jnp.float32) + dec_bias_ref[...]
        rebuilt[here] = whole
        row = start + lax.broadcasted_iota(jnp.int32, whole.shape, 0)
        error = whole - targets[here].astype(jnp.float32)
        residual[here] = jnp.where(row < live_ref[base + b], error, 0.0).astype(jnp.bfloat16)

    load_live.wait()
    load_bias.wait()
    load_act.wait()
    load_enc.wait()
    encode(me)
    t1(me, me).start()
    s1(twin).wait_recv()
    encode(twin)
    t1(me, twin).start()
    load_dec.wait()
    load_targets.wait()
    load_dec_bias.wait()
    t1(twin, home).wait_recv()
    t1(twin, home + 1).wait_recv()

    def home_step(i, carry):
        home_features(home + i)
        return carry

    lax.fori_loop(0, 2, home_step, 0)

    for h in range(len(act_cuts)):
        s2(peer, h).wait_recv()
        s3(peer, h).start()
    for h in range(len(act_cuts)):
        s2(me, h).wait_send()
    for b in (home, home + 1):
        for h in every:
            t2(me, b, h).start()
    encode(peer)
    t1(me, peer).start()
    for h in range(len(act_cuts)):
        s3(peer_twin, h).wait_recv()
    encode(peer_twin)
    t1(me, peer_twin).start()
    for b in (away, away + 1):
        for h in every:
            t2(me, b, h).start()
    t1(twin, away).wait_recv()
    t1(twin, away + 1).wait_recv()

    def away_step(i, carry):
        home_features(away + i)
        return carry

    lax.fori_loop(0, 2, away_step, 0)

    def finish_step(i, carry):
        for h in every:
            finish(lax.rem(away + i, 4), h)
        return carry

    lax.fori_loop(0, 4, finish_step, 0)

    s1(me).wait_send()
    for h in range(len(act_cuts)):
        s3(peer, h).wait_send()
    for b in range(4):
        t1(me, b).wait_send()
        for h in every:
            t2(me, b, h).wait_send()
            t3(peer, b, h).wait_send()


def gradient_kernel(span, codes_ref, residual_ref, rebuilt_ref, rebuilt_hbm, grad_hbm, grad, sem):
    owners, width = codes_ref.shape[0], codes_ref.shape[2]
    per = width // span
    copies = [pltpu.make_async_copy(rebuilt_ref, rebuilt_hbm, sem.at[owners * per])]
    copies[0].start()
    for i in range(owners * per):
        at = pl.ds(i % per * span, span)
        grad[i // per, at] = lax.dot_general(
            codes_ref[i // per, :, at],
            residual_ref[...],
            (((0,), (0,)), ((), ())),
            preferred_element_type=jnp.float32,
        )
        copy = pltpu.make_async_copy(grad.at[i // per, at], grad_hbm.at[i // per, at], sem.at[i])
        copy.start()
        copies.append(copy)
    for copy in copies:
        copy.wait()


def four_owners(
    activations, live_rows, encoder_weight, encoder_bias, decoder_weight, decoder_bias, targets
):
    rows, depth = activations.shape
    features = encoder_weight.shape[1]
    width = decoder_weight.shape[2]
    tokens = targets.shape[0]
    act_cuts = cuts(rows, (1, 1))
    code_cuts = cuts(rows, (5, 3, 2))
    any_space = pl.BlockSpec(memory_space=pl.ANY)
    stay = functools.partial(pltpu.with_memory_space_constraint, memory_space=pltpu.HBM)
    in_vmem = pl.BlockSpec(memory_space=pltpu.VMEM)
    in_hbm = pl.BlockSpec(memory_space=pltpu.HBM)
    dma = pltpu.SemaphoreType.DMA
    bf16 = jnp.bfloat16
    codes, residual, rebuilt = pl.pallas_call(
        functools.partial(gather_kernel, act_cuts, code_cuts),
        out_shape=(
            pltpu.VMEM((4, tokens, features), bf16),
            pltpu.VMEM((tokens, width), bf16),
            pltpu.VMEM((tokens, width), jnp.float32),
        ),
        in_specs=[in_hbm] * 7,
        out_specs=(in_vmem, in_vmem, in_vmem),
        scratch_shapes=[
            pltpu.VMEM((4, rows, depth), bf16),
            pltpu.VMEM((depth, features), bf16),
            pltpu.VMEM((4, features, width), bf16),
            pltpu.VMEM((tokens, width), jnp.float32),
            pltpu.VMEM((tokens, width), bf16),
            pltpu.SMEM(live_rows.shape, jnp.int32),
            pltpu.VMEM((1, features), jnp.float32),
            pltpu.VMEM((1, width), jnp.float32),
            dma((7,)),
            dma((1,)),
            dma((1,)),
            dma((len(act_cuts),)),
            dma((len(act_cuts),)),
            dma((len(act_cuts),)),
            dma((len(act_cuts),)),
            dma((4,)),
            dma((4,)),
            dma((4, len(code_cuts))),
            dma((4, len(code_cuts))),
            dma((4, len(code_cuts))),
            dma((4, len(code_cuts))),
        ],
        compiler_params=pltpu.CompilerParams(
            collective_id=0, has_side_effects=True, vmem_limit_bytes=44 * 1024 * 1024
        ),
        name="gather_codes",
    )(
        activations,
        stay(live_rows),
        encoder_weight,
        stay(encoder_bias[None, :]),
        decoder_weight,
        stay(decoder_bias[None, :]),
        targets,
    )

    span = min(256, features)
    rebuilt, grad = pl.pallas_call(
        functools.partial(gradient_kernel, span),
        out_shape=(
            jax.ShapeDtypeStruct((tokens, width), jnp.float32),
            jax.ShapeDtypeStruct((4, features, width), jnp.float32),
        ),
        in_specs=[in_vmem, in_vmem, in_vmem],
        out_specs=(any_space, any_space),
        scratch_shapes=[
            pltpu.VMEM((4, features, width), jnp.float32),
            dma((4 * (features // span) + 1,)),
        ],
        compiler_params=pltpu.CompilerParams(vmem_limit_bytes=44 * 1024 * 1024),
        name="gradient",
    )(codes, residual, rebuilt)
    return rebuilt, grad


def from_partner(shard, axis, distance):
    return lax.ppermute(shard, axis, [(i, i ^ 1 << distance) for i in range(lax.axis_size(axis))])


def group_rows(block, levels, position):
    for bit in range(levels):
        other = from_partner(block, "blk", bit)
        upper = position >> bit & 1 == 1
        block = jnp.where(
            upper, jnp.concatenate([other, block], 0), jnp.concatenate([block, other], 0)
        )
    return block


def general(
    activations, live_rows, encoder_weight, encoder_bias, decoder_weight, decoder_bias, targets
):
    owners = lax.axis_size("blk") // G
    levels = owners.bit_length() - 1
    shares = lax.axis_size("feat")
    position = lax.axis_index("blk")
    share_index = lax.axis_index("feat")
    group_index = position // owners
    tok_rows = activations.shape[0]
    counts = lax.dynamic_slice_in_dim(live_rows, group_index * owners, owners)
    positions = jnp.arange(tok_rows, dtype=jnp.int32)
    live_mask = (positions[None, :] < counts[:, None]).astype(jnp.float32).reshape(-1)
    gathered = group_rows(activations, levels, position)
    per_share = encoder_weight.shape[1] // shares
    bias_share = lax.dynamic_slice_in_dim(encoder_bias, share_index * per_share, per_share)
    columns = encoder_weight
    whole = lax.psum(
        lax.dot_general(
            columns, gathered, (((0,), (1,)), ((), ())), preferred_element_type=jnp.float32
        ).astype(jnp.bfloat16),
        "feat",
    ).astype(jnp.float32)
    preact = lax.dynamic_slice_in_dim(whole, share_index * per_share, per_share, 0)
    codes_by_feature = (jax.nn.relu(preact + bias_share[:, None]) * live_mask[None, :]).astype(
        jnp.bfloat16
    )
    codes_all = group_rows(codes_by_feature, levels, position)
    decoder_rows = decoder_weight.reshape(-1, decoder_weight.shape[2])
    block_rows = gathered.shape[0] // shares
    columns = codes_all
    summed = lax.psum_scatter(
        lax.dot_general(
            columns, decoder_rows, (((0,), (0,)), ((), ())), preferred_element_type=jnp.float32
        ).astype(jnp.bfloat16),
        "feat",
        scatter_dimension=0,
        tiled=True,
    ).astype(jnp.float32)
    rebuilt = summed + decoder_bias[None, :]
    mask_block = lax.dynamic_slice_in_dim(live_mask, share_index * block_rows, block_rows)
    residual = ((rebuilt - targets.astype(jnp.float32)) * mask_block[:, None]).astype(jnp.bfloat16)
    columns = codes_all
    gradient = jnp.dot(
        columns,
        lax.all_gather(residual, "feat", axis=0, tiled=True),
        preferred_element_type=jnp.float32,
    )
    return (rebuilt, gradient.reshape(decoder_weight.shape))


def solution(mesh):
    in_specs = (
        P("blk", "feat"),
        P(),
        P("feat", "blk"),
        P("blk"),
        P(None, "feat", "blk"),
        P("blk"),
        P("feat", "blk"),
    )
    out_specs = (P("feat", "blk"), P(None, "feat", "blk"))
    fused = mesh.shape["blk"] // G == 4 and mesh.shape["feat"] == 1
    return jax.shard_map(
        four_owners if fused else general,
        mesh=mesh,
        in_specs=in_specs,
        out_specs=out_specs,
        check_vma=False,
    )
```

time: 80.1 us -> 73.7 us (0.920)
  Pallas kernels: 78.9 us -> 72.5 us
    pallas_call x2, Pallas kernels: 78.9 us -> 72.5 us  [the longest x1 64.7 us: four_owners(): pl.pallas_call(functools.partial(gather_kernel, act_cuts, code_cuts), out...]
where the time goes in v1:
time: 73.7 us; the launch traced here: 73.2 us
  Pallas kernels  72.5 us (98%)
    pallas_call x1, Pallas kernels, four_owners(): pl.pallas_call(functools.partial(gather_kernel, act_cuts, code_cuts), out...  64.7 us
    pallas_call x1, Pallas kernels, four_owners(): pl.pallas_call(functools.partial(gradient_kernel, span), out_shape=(jax.S...  7.84 us

profile of v1, /device:TPU:0, one launch (start us, length us, event | category | flops | bytes accessed | tf_op | source)
XLA Modules:
  0.0 73.2 jit_solution(6644680654540180920)
XLA Ops:
  0.6 64.7 %gather_codes.1 = (bf16[4,640,1024]{2,1,0:T(8,128)(2,1)S(1)}, bf16[640,1024]{1,0:T(8,128)(2,1)S(1)}, f32[640,1024]{1,0:T(8,128)S(1)}) custom-call(bf16[160,4096]{1,0:T(8,128)(2,1)} %act_hbm.1, s32[32]{0:T(128)} %live_hbm.1, bf16[4096,1024]{1,0:T(8,128)(2,1)} %enc_hbm.1, f32[1,1024]{1,0:T(1,128)} %bitcast.2, bf16[4,1024,1024]{2,1,0:T(8,128)(2,1)} %dec_hbm.1, ...), custom_call_target="tpu_custom_call" | custom-call | tf_op jit(solution)/shard_map/gather_codes/pallas_call | solution.py:283
  65.3 7.8 %gradient.1 = (f32[640,1024]{1,0:T(8,128)}, f32[4,1024,1024]{2,1,0:T(8,128)}) custom-call(bf16[4,640,1024]{2,1,0:T(8,128)(2,1)S(1)} %get-tuple-element.5.codes_ref, bf16[640,1024]{1,0:T(8,128)(2,1)S(1)} %get-tuple-element.6.residual_ref, f32[640,1024]{1,0:T(8,128)S(1)} %get-tuple-element.7.rebuilt_ref), custom_call_target="tpu_custom_call" | custom-call | tf_op jit(solution)/shard_map/gradient/pallas_call | solution.py:330

commit v2 on v1

--- a/solution.py
+++ b/solution.py
@@ -190,6 +190,9 @@
     s1(twin).wait_recv()
     encode(twin)
     t1(me, twin).start()
+    for b in (home, home + 1):
+        for h in every:
+            t2(me, b, h).start()
     load_dec.wait()
     load_targets.wait()
     load_dec_bias.wait()
@@ -205,11 +208,6 @@
     for h in range(len(act_cuts)):
         s2(peer, h).wait_recv()
         s3(peer, h).start()
-    for h in range(len(act_cuts)):
-        s2(me, h).wait_send()
-    for b in (home, home + 1):
-        for h in every:
-            t2(me, b, h).start()
     encode(peer)
     t1(me, peer).start()
     for h in range(len(act_cuts)):
@@ -236,6 +234,8 @@
     lax.fori_loop(0, 4, finish_step, 0)
 
     s1(me).wait_send()
+    for h in range(len(act_cuts)):
+        s2(me, h).wait_send()
     for h in range(len(act_cuts)):
         s3(peer, h).wait_send()
     for b in range(4):

time: 73.7 us -> 71.9 us (0.976)
  Pallas kernels: 72.5 us -> 71.1 us
    pallas_call x1, Pallas kernels: 64.7 us -> 63.3 us  [four_owners(): pl.pallas_call(functools.partial(gather_kernel, act_cuts, code_cuts), out...]
where the time goes in v2:
time: 71.9 us; the launch traced here: 71.8 us
  Pallas kernels  71.1 us (99%)
    pallas_call x1, Pallas kernels, four_owners(): pl.pallas_call(functools.partial(gather_kernel, act_cuts, code_cuts), out...  63.3 us
    pallas_call x1, Pallas kernels, four_owners(): pl.pallas_call(functools.partial(gradient_kernel, span), out_shape=(jax.S...  7.84 us

profile of v2, /device:TPU:0, one launch (start us, length us, event | category | flops | bytes accessed | tf_op | source)
XLA Modules:
  0.0 71.8 jit_solution(11996966684839323416)
XLA Ops:
  0.6 63.3 %gather_codes.1 = (bf16[4,640,1024]{2,1,0:T(8,128)(2,1)S(1)}, bf16[640,1024]{1,0:T(8,128)(2,1)S(1)}, f32[640,1024]{1,0:T(8,128)S(1)}) custom-call(bf16[160,4096]{1,0:T(8,128)(2,1)} %act_hbm.1, s32[32]{0:T(128)} %live_hbm.1, bf16[4096,1024]{1,0:T(8,128)(2,1)} %enc_hbm.1, f32[1,1024]{1,0:T(1,128)} %bitcast.2, bf16[4,1024,1024]{2,1,0:T(8,128)(2,1)} %dec_hbm.1, ...), custom_call_target="tpu_custom_call" | custom-call | tf_op jit(solution)/shard_map/gather_codes/pallas_call | solution.py:283
  63.9 7.8 %gradient.1 = (f32[640,1024]{1,0:T(8,128)}, f32[4,1024,1024]{2,1,0:T(8,128)}) custom-call(bf16[4,640,1024]{2,1,0:T(8,128)(2,1)S(1)} %get-tuple-element.5.codes_ref, bf16[640,1024]{1,0:T(8,128)(2,1)S(1)} %get-tuple-element.6.residual_ref, f32[640,1024]{1,0:T(8,128)S(1)} %get-tuple-element.7.rebuilt_ref), custom_call_target="tpu_custom_call" | custom-call | tf_op jit(solution)/shard_map/gradient/pallas_call | solution.py:330

commit v3 on v2

v3 whole, which is shorter than its diff:
```python
import functools

import jax
import jax.numpy as jnp
from jax import lax
from jax.experimental import pallas as pl
from jax.experimental.pallas import tpu as pltpu
from jax.sharding import PartitionSpec as P

G = 8
TILE = 16
MESH = pl.DeviceIdType.MESH


def cuts(rows, parts):
    if rows % 16 or rows // 16 < len(parts):
        return [(0, rows)]
    tiles, total, edges = rows // 16, sum(parts), [0]
    for k in range(1, len(parts)):
        edges.append(max(edges[-1] + 1, tiles * sum(parts[:k]) // total))
    edges.append(tiles)
    return [(16 * a, 16 * (b - a)) for a, b in zip(edges[:-1], edges[1:])]


def pieces_of(early, rest):
    first = [(0, *cut) for cut in cuts(early, (1, 1))]
    if rest:
        return first + [(1, 0, early)] + [(2, *cut) for cut in cuts(rest, (5, 3, 2))]
    return first + [(1, *cut) for cut in cuts(early, (5, 3, 2))]


def step(count):
    return jnp.clip(count, 0, 1)


def tile_of(first_live, second_live, tiles, k):
    first = first_live + TILE - 1 >> 4
    second = second_live + TILE - 1 >> 4
    late = 1 - step(first - k)
    inside = jnp.minimum(k - late * first, tiles - 1)
    live = first_live + late * (second_live - first_live) - TILE * inside
    return inside + late * tiles, step(first + second - k) * live


def gather_kernel(
    act_cuts,
    early,
    pieces,
    act_hbm,
    live_hbm,
    enc_hbm,
    bias_hbm,
    dec_hbm,
    dec_bias_hbm,
    targets_hbm,
    codes,
    residual,
    summed,
    acts_home,
    acts_away,
    packed,
    enc,
    dec,
    part,
    targets,
    packed_targets,
    keep,
    live_ref,
    bias_ref,
    dec_bias_ref,
    load_sem,
    s1_send,
    s1_recv,
    s2_send,
    s2_recv,
    s3_send,
    s3_recv,
    t1_send,
    t1_recv,
    t2_send,
    t2_recv,
    t3_send,
    t3_recv,
):
    position = lax.axis_index("blk")
    share = lax.axis_index("feat")
    base = position // 4 * 4
    me = position % 4
    core = me % 2
    home = me - core
    away = 2 - home
    chip = home // 2
    other = 1 - chip
    twin = home + 1 - core
    peer = away + core
    peer_twin = away + 1 - core
    on_chip = (base + twin, share)
    across = (base + peer, share)

    block_tiles = act_hbm.shape[0]
    total = codes.shape[1]
    rest = total - 2 * early
    width = enc.shape[1]
    column_tile = min(256, width)
    columns = width // column_tile

    def own_tiles(at_core, start, count):
        return pl.ds(at_core * block_tiles + start, count)

    load_act = pltpu.make_async_copy(
        act_hbm, acts_home.at[own_tiles(core, 0, block_tiles)], load_sem.at[0]
    )
    load_enc = pltpu.make_async_copy(enc_hbm, enc, load_sem.at[1])
    load_dec = pltpu.make_async_copy(dec_hbm, dec, load_sem.at[2])
    load_targets = pltpu.make_async_copy(targets_hbm, targets, load_sem.at[3])
    load_live = pltpu.make_async_copy(live_hbm, live_ref, load_sem.at[4])
    load_bias = pltpu.make_async_copy(bias_hbm, bias_ref, load_sem.at[5])
    load_dec_bias = pltpu.make_async_copy(dec_bias_hbm, dec_bias_ref, load_sem.at[6])
    load_live.start()
    load_bias.start()
    load_act.start()
    load_enc.start()
    load_dec_bias.start()

    barrier = pltpu.get_barrier_semaphore()
    for neighbour in (on_chip, across):
        pl.semaphore_signal(barrier, inc=1, device_id=neighbour, device_id_type=MESH)
    pl.semaphore_wait(barrier, 2)

    def remote(src, dst, send, recv, to):
        return pltpu.make_async_remote_copy(
            src_ref=src,
            dst_ref=dst,
            send_sem=send,
            recv_sem=recv,
            device_id=to,
            device_id_type=MESH,
        )

    def s1(at_core):
        ref = acts_home.at[own_tiles(at_core, 0, block_tiles)]
        return remote(act_hbm, ref, s1_send.at[0], s1_recv.at[0], on_chip)

    def s2(h):
        ref = acts_away.at[own_tiles(core, *act_cuts[h])]
        return remote(act_hbm.at[pl.ds(*act_cuts[h])], ref, s2_send.at[h], s2_recv.at[h], across)

    def s3(at_core, h):
        ref = acts_away.at[own_tiles(at_core, *act_cuts[h])]
        return remote(ref, ref, s3_send.at[h], s3_recv.at[h], on_chip)

    def region(kind, of_chip, start, count):
        first = (of_chip * early, (1 - of_chip) * early, 2 * early)[kind]
        return pl.ds(pl.multiple_of(first + start, TILE), count)

    sizes = (early, early, rest)
    kinds = (0, 1, 2) if rest else (0, 1)

    def t1(f, kind):
        ref = codes.at[f, region(kind, chip, 0, sizes[kind])]
        return remote(ref, ref, t1_send.at[kind], t1_recv.at[kind], on_chip)

    def t2(f, p, of_chip):
        kind, start, count = pieces[p]
        ref = codes.at[f, region(kind, of_chip, start, count)]
        return remote(ref, ref, t2_send.at[p], t2_recv.at[p], across)

    def t3(f, p):
        kind, start, count = pieces[p]
        ref = codes.at[f, region(kind, other, start, count)]
        return remote(ref, ref, t3_send.at[p], t3_recv.at[p], on_chip)

    def send(kind):
        t1(me, kind).start()
        for p, piece in enumerate(pieces):
            if piece[0] == kind:
                t2(me, p, chip).start()

    for h in range(len(act_cuts)):
        s2(h).start()
    s1(core).start()
    load_dec.start()
    load_targets.start()

    def mark(at, live, where):
        keep[at] = (lax.broadcasted_iota(jnp.int32, (TILE, keep.shape[1]), 0) < live).astype(
            jnp.float32
        )
        packed_targets[at] = targets[where]

    def pack(acts, of_chip):
        first_live = live_ref[base + 2 * of_chip]
        second_live = live_ref[base + 2 * of_chip + 1]

        def one(k, carry):
            where, live = tile_of(first_live, second_live, block_tiles, k)
            at = pl.ds(pl.multiple_of(of_chip * early + k * TILE, TILE), TILE)
            packed[at] = acts[where]
            mark(at, live, of_chip * 2 * block_tiles + where)
            return carry

        lax.fori_loop(0, early // TILE, one, 0)

    def pack_rest():
        lives = [live_ref[base + b] for b in range(4)]
        first_extra = jnp.maximum(
            (lives[0] + TILE - 1 >> 4) + (lives[1] + TILE - 1 >> 4) - early // TILE, 0
        )

        def one(k, carry):
            from_first = step(first_extra - k)
            index = early // TILE + k - (1 - from_first) * first_extra
            where0, live0 = tile_of(lives[0], lives[1], block_tiles, index)
            where1, live1 = tile_of(lives[2], lives[3], block_tiles, index)
            where_home = where0 + chip * (where1 - where0)
            where_away = where1 + chip * (where0 - where1)
            at = pl.ds(pl.multiple_of(2 * early + k * TILE, TILE), TILE)
            mine = jnp.full((TILE, acts_home.shape[2]), from_first + chip, jnp.int32) == 1
            packed[at] = jnp.where(mine, acts_home[where_home], acts_away[where_away])
            mark(
                at,
                live1 + from_first * (live0 - live1),
                where1 + 2 * block_tiles + from_first * (where0 - where1 - 2 * block_tiles),
            )
            return carry

        lax.fori_loop(0, rest // TILE, one, 0)

    def encode(kind):
        here = region(kind, chip, 0, sizes[kind])

        def column(n, carry):
            at = pl.ds(pl.multiple_of(n * column_tile, column_tile), column_tile)
            product = jnp.dot(packed[here], enc[:, at], preferred_element_type=jnp.float32)
            value = product.astype(jnp.bfloat16).astype(jnp.float32) + bias_ref[:, at]
            codes[me, here, at] = jnp.maximum(value, 0.0).astype(jnp.bfloat16)
            return carry

        lax.fori_loop(0, columns, column, 0)

    def home_features(kind):
        here = region(kind, chip, 0, sizes[kind])

        def column(n, carry):
            at = pl.ds(pl.multiple_of(n * column_tile, column_tile), column_tile)
            first = jnp.dot(
                codes[me, here], dec[me, :, at], preferred_element_type=jnp.float32
            )
            second = jnp.dot(
                codes[twin, here], dec[twin, :, at], preferred_element_type=jnp.float32
            )
            part[here, at] = first + second
            return carry

        lax.fori_loop(0, columns, column, 0)

    def finish(p):
        kind, start, count = pieces[p]
        here = region(kind, other, start, count)
        step = column_tile if count > 64 else width

        def add(f):
            def column(n, carry):
                at = pl.ds(pl.multiple_of(n * step, step), step)
                part[here, at] += jnp.dot(
                    codes[f, here], dec[f, :, at], preferred_element_type=jnp.float32
                )
                return carry

            lax.fori_loop(0, width // step, column, 0)

        t2(peer, p, other).wait_recv()
        t3(peer, p).start()
        add(peer)
        t3(peer_twin, p).wait_recv()
        add(peer_twin)
        whole = part[here].astype(jnp.bfloat16)
        summed[here] = whole
        error = (
            whole.astype(jnp.float32)
            + dec_bias_ref[...]
            - packed_targets[here].astype(jnp.float32)
        )
        live = jnp.concatenate([keep[here]] * (width // keep.shape[1]), axis=1)
        residual[here] = jnp.where(live > 0.0, error, 0.0).astype(jnp.bfloat16)

    load_live.wait()
    load_bias.wait()
    load_dec_bias.wait()
    load_act.wait()
    s1(1 - core).wait_recv()
    load_targets.wait()
    pack(acts_home, chip)
    load_enc.wait()
    encode(0)
    send(0)
    load_dec.wait()
    t1(twin, 0).wait_recv()
    home_features(0)

    for h in range(len(act_cuts)):
        s2(h).wait_recv()
        s3(core, h).start()
    for h in range(len(act_cuts)):
        s3(1 - core, h).wait_recv()
    pack(acts_away, other)
    encode(1)
    send(1)
    if rest:
        pack_rest()
        encode(2)
        send(2)
    for kind in kinds[1:]:
        t1(twin, kind).wait_recv()
        home_features(kind)
    for p in range(len(pieces)):
        finish(p)

    s1(core).wait_send()
    for h in range(len(act_cuts)):
        s2(h).wait_send()
        s3(core, h).wait_send()
    for kind in kinds:
        t1(me, kind).wait_send()
    for p in range(len(pieces)):
        t2(me, p, chip).wait_send()
        t3(peer, p).wait_send()


def gradient_kernel(
    span,
    early,
    live_ref,
    codes_ref,
    residual_ref,
    summed_ref,
    bias_ref,
    rebuilt_hbm,
    grad_hbm,
    grad,
    rebuilt,
    sem,
):
    owners, width = codes_ref.shape[0], codes_ref.shape[2]
    block_tiles = rebuilt.shape[0] // TILE // 4
    base = lax.axis_index("blk") // 4 * 4
    per = width // span

    def out(f, i):
        at = pl.ds(pl.multiple_of(i * span, span), span)
        return pltpu.make_async_copy(grad.at[f, at], grad_hbm.at[f, at], sem.at[f * per + i])

    def block(f, i):
        at = pl.ds(i * span, span)
        grad[f, at] = lax.dot_general(
            codes_ref[f, :, at],
            residual_ref[...],
            (((0,), (0,)), ((), ())),
            preferred_element_type=jnp.float32,
        )
        out(f, i).start()

    lives = [live_ref[base + b] for b in range(4)]
    counts = [live + TILE - 1 >> 4 for live in lives]
    first_extra = jnp.maximum(counts[0] + counts[1] - early // TILE, 0)

    def spread(b):
        chip = b // 2
        before = counts[b - 1] if b % 2 else 0

        def one(s, carry):
            k = before + s
            place = jnp.where(
                k < early // TILE,
                chip * (early // TILE) + k,
                early // TILE + chip * first_extra + k,
            )
            place = jnp.where(s < counts[b], place, 0)
            value = summed_ref[pl.ds(pl.multiple_of(place * TILE, TILE), TILE)].astype(jnp.float32)
            row = TILE * s + lax.broadcasted_iota(jnp.int32, value.shape, 0)
            at = pl.ds(pl.multiple_of((b * block_tiles + s) * TILE, TILE), TILE)
            rebuilt[at] = jnp.where(row < lives[b], value, 0.0) + bias_ref[...]
            return carry

        lax.fori_loop(0, block_tiles, one, 0)

    def owner(f, carry):
        for i in range(per):
            block(f, i)
        return carry

    lax.fori_loop(0, owners // 2, owner, 0)
    for b in range(4):
        spread(b)
    give = pltpu.make_async_copy(rebuilt, rebuilt_hbm, sem.at[owners * per])
    give.start()
    lax.fori_loop(owners // 2, owners, owner, 0)

    def ended(i, carry):
        out(i // per, i % per).wait()
        return carry

    lax.fori_loop(0, owners * per, ended, 0)
    give.wait()


def packed_tiles(
    order,
    tiles,
    activations,
    live_rows,
    encoder_weight,
    encoder_bias,
    decoder_weight,
    decoder_bias,
    targets,
):
    rows, depth = activations.shape
    features = encoder_weight.shape[1]
    width = decoder_weight.shape[2]
    tokens = targets.shape[0]
    total = TILE * tiles
    early = total - 2 * rows
    block_tiles = rows // TILE
    half = (block_tiles + 1) // 2
    act_cuts = [(0, half), (half, block_tiles - half)]
    act_cuts = [cut for cut in act_cuts if cut[1]]
    pieces = pieces_of(early, total - 2 * early)
    lanes = min(128, width)
    any_space = pl.BlockSpec(memory_space=pl.ANY)
    stay = functools.partial(pltpu.with_memory_space_constraint, memory_space=pltpu.HBM)
    in_vmem = pl.BlockSpec(memory_space=pltpu.VMEM)
    in_smem = pl.BlockSpec(memory_space=pltpu.SMEM)
    in_hbm = pl.BlockSpec(memory_space=pltpu.HBM)
    dma = pltpu.SemaphoreType.DMA
    bf16 = jnp.bfloat16
    f32 = jnp.float32
    codes, residual, summed = pl.pallas_call(
        functools.partial(gather_kernel, act_cuts, early, pieces),
        out_shape=(
            pltpu.VMEM((4, total, features), bf16),
            pltpu.VMEM((total, width), bf16),
            pltpu.VMEM((total, width), bf16),
        ),
        in_specs=[in_hbm] * 7,
        out_specs=(in_vmem, in_vmem, in_vmem),
        scratch_shapes=[
            pltpu.VMEM((2 * block_tiles, TILE, depth), bf16),
            pltpu.VMEM((2 * block_tiles, TILE, depth), bf16),
            pltpu.VMEM((total, depth), bf16),
            pltpu.VMEM((depth, features), bf16),
            pltpu.VMEM((4, features, width), bf16),
            pltpu.VMEM((total, width), f32),
            pltpu.VMEM((4 * block_tiles, TILE, width), bf16),
            pltpu.VMEM((total, width), bf16),
            pltpu.VMEM((total, lanes), f32),
            pltpu.SMEM(live_rows.shape, jnp.int32),
            pltpu.VMEM((1, features), f32),
            pltpu.VMEM((1, width), f32),
            dma((7,)),
            dma((1,)),
            dma((1,)),
            dma((len(act_cuts),)),
            dma((len(act_cuts),)),
            dma((len(act_cuts),)),
            dma((len(act_cuts),)),
            dma((3,)),
            dma((3,)),
            dma((len(pieces),)),
            dma((len(pieces),)),
            dma((len(pieces),)),
            dma((len(pieces),)),
        ],
        compiler_params=pltpu.CompilerParams(
            collective_id=order, has_side_effects=True, vmem_limit_bytes=44 * 1024 * 1024
        ),
        name=f"gather_codes_{tiles}",
    )(
        activations.reshape(block_tiles, TILE, depth),
        stay(live_rows),
        encoder_weight,
        stay(encoder_bias[None, :]),
        decoder_weight,
        stay(decoder_bias[None, :]),
        targets.reshape(4 * block_tiles, TILE, width),
    )

    span = min(256, features)
    rebuilt, grad = pl.pallas_call(
        functools.partial(gradient_kernel, span, early),
        out_shape=(
            jax.ShapeDtypeStruct((tokens, width), f32),
            jax.ShapeDtypeStruct((4, features, width), f32),
        ),
        in_specs=[in_smem, in_vmem, in_vmem, in_vmem, in_vmem],
        out_specs=(any_space, any_space),
        scratch_shapes=[
            pltpu.VMEM((4, features, width), f32),
            pltpu.VMEM((tokens, width), f32),
            dma((4 * (features // span) + 1,)),
        ],
        compiler_params=pltpu.CompilerParams(vmem_limit_bytes=44 * 1024 * 1024),
        name=f"gradient_{tiles}",
    )(live_rows, codes, residual, summed, decoder_bias[None, :])
    return rebuilt, grad


def four_owners(activations, live_rows, *operands):
    rows = activations.shape[0]
    if rows % TILE:
        return general(activations, live_rows, *operands)
    block_tiles = rows // TILE
    sizes = sorted({2 * block_tiles + max(1, block_tiles * k // 10) for k in (9, 12, 15, 20)})
    most = (live_rows + TILE - 1 >> 4).reshape(-1, 4).sum(1).max()
    choice = sum((most > size).astype(jnp.int32) for size in sizes[:-1])
    return lax.switch(
        choice,
        [functools.partial(packed_tiles, order, tiles) for order, tiles in enumerate(sizes)],
        activations,
        live_rows,
        *operands,
    )


def from_partner(shard, axis, distance):
    return lax.ppermute(shard, axis, [(i, i ^ 1 << distance) for i in range(lax.axis_size(axis))])


def group_rows(block, levels, position):
    for bit in range(levels):
        other = from_partner(block, "blk", bit)
        upper = position >> bit & 1 == 1
        block = jnp.where(
            upper, jnp.concatenate([other, block], 0), jnp.concatenate([block, other], 0)
        )
    return block


def general(
    activations, live_rows, encoder_weight, encoder_bias, decoder_weight, decoder_bias, targets
):
    owners = lax.axis_size("blk") // G
    levels = owners.bit_length() - 1
    shares = lax.axis_size("feat")
    position = lax.axis_index("blk")
    share_index = lax.axis_index("feat")
    group_index = position // owners
    tok_rows = activations.shape[0]
    counts = lax.dynamic_slice_in_dim(live_rows, group_index * owners, owners)
    positions = jnp.arange(tok_rows, dtype=jnp.int32)
    live_mask = (positions[None, :] < counts[:, None]).astype(jnp.float32).reshape(-1)
    gathered = group_rows(activations, levels, position)
    per_share = encoder_weight.shape[1] // shares
    bias_share = lax.dynamic_slice_in_dim(encoder_bias, share_index * per_share, per_share)
    columns = encoder_weight
    whole = lax.psum(
        lax.dot_general(
            columns, gathered, (((0,), (1,)), ((), ())), preferred_element_type=jnp.float32
        ).astype(jnp.bfloat16),
        "feat",
    ).astype(jnp.float32)
    preact = lax.dynamic_slice_in_dim(whole, share_index * per_share, per_share, 0)
    codes_by_feature = (jax.nn.relu(preact + bias_share[:, None]) * live_mask[None, :]).astype(
        jnp.bfloat16
    )
    codes_all = group_rows(codes_by_feature, levels, position)
    decoder_rows = decoder_weight.reshape(-1, decoder_weight.shape[2])
    block_rows = gathered.shape[0] // shares
    columns = codes_all
    summed = lax.psum_scatter(
        lax.dot_general(
            columns, decoder_rows, (((0,), (0,)), ((), ())), preferred_element_type=jnp.float32
        ).astype(jnp.bfloat16),
        "feat",
        scatter_dimension=0,
        tiled=True,
    ).astype(jnp.float32)
    rebuilt = summed + decoder_bias[None, :]
    mask_block = lax.dynamic_slice_in_dim(live_mask, share_index * block_rows, block_rows)
    residual = ((rebuilt - targets.astype(jnp.float32)) * mask_block[:, None]).astype(jnp.bfloat16)
    columns = codes_all
    gradient = jnp.dot(
        columns,
        lax.all_gather(residual, "feat", axis=0, tiled=True),
        preferred_element_type=jnp.float32,
    )
    return (rebuilt, gradient.reshape(decoder_weight.shape))


def solution(mesh):
    in_specs = (
        P("blk", "feat"),
        P(),
        P("feat", "blk"),
        P("blk"),
        P(None, "feat", "blk"),
        P("blk"),
        P("feat", "blk"),
    )
    out_specs = (P("feat", "blk"), P(None, "feat", "blk"))
    fused = mesh.shape["blk"] // G == 4 and mesh.shape["feat"] == 1
    return jax.shard_map(
        four_owners if fused else general,
        mesh=mesh,
        in_specs=in_specs,
        out_specs=out_specs,
        check_vma=False,
    )
```

time: 71.9 us -> 69.6 us (0.968); the launches traced: 71.8 us -> 68.4 us
  Pallas kernels: 71.1 us -> 63.3 us
  between operations: 0.64 us -> 2.8 us
  other arithmetic: 0 us -> 1.42 us
  loops' own time: 0 us -> 0.77 us
    pallas_call x2, Pallas kernels: 71.1 us -> 63.3 us  [the longest x1 55.5 us: packed_tiles(): pl.pallas_call(functools.partial(gather_kernel, act_cuts, early, pieces),...]
    another operation x0 -> x1, loops' own time: none -> 0.77 us  [four_owners(): lax.switch(choice, [functools.partial(packed_tiles, order, tiles) for ord...]
where the time goes in v3:
time: 69.6 us; the launch traced here: 68.4 us
  Pallas kernels  63.3 us (91%)
  between operations  2.8 us (4%)
  other arithmetic  1.42 us (2%)
  loops' own time  0.77 us (1%)
    pallas_call x1, Pallas kernels, packed_tiles(): pl.pallas_call(functools.partial(gather_kernel, act_cuts, early, pieces),...  55.5 us
    pallas_call x1, Pallas kernels, packed_tiles(): pl.pallas_call(functools.partial(gradient_kernel, span, early), out_shape...  7.82 us

profile of v3, /device:TPU:0, one launch (start us, length us, event | category | flops | bytes accessed | tf_op | source)
XLA Modules:
  0.0 68.4 jit_solution(1488655939409536654)
XLA Ops:
  0.6 0.7 add_shift-right-arithmetic_fusion
  1.3 0.1 reshape.31
  1.4 0.1 reduce_sum.9
  1.5 0.6 reduce_max.9
  4.1 64.1 %conditional.1 = ((f32[640,1024]{1,0:T(8,128)}, f32[4,1024,1024]{2,1,0:T(8,128)})) conditional(s32[]{:T(128)} %clamp.3, (bf16[160,4096]{1,0:T(8,128)(2,1)}, f32[1024]{0:T(1024)}, f32[1024]{0:T(1024)}, bf16[640,1024]{1,0:T(8,128)(2,1)}, s32[32]{0:T(128)}, /*index=5*/bf16[4096,1024]{1,0:T(8,128)(2,1)}, ...), branch_computations={%region_2.0_spmd, %region_3.0_spmd, %region_4.0_spmd, %region_5.0_... | conditional | bytes 16960 | solution.py:516
  4.1 0.0 copy-start
  4.1 0.0 copy-start.4
  4.1 55.5 %gather_codes_29.1 = (bf16[4,464,1024]{2,1,0:T(8,128)(2,1)S(1)}, bf16[464,1024]{1,0:T(8,128)(2,1)S(1)}, bf16[464,1024]{1,0:T(8,128)(2,1)S(1)}) custom-call(bf16[10,16,4096]{2,1,0:T(8,128)(2,1)} %bitcast.16, s32[32]{0:T(128)} %get-tuple-element.56.live_hbm.live_ref, bf16[4096,1024]{1,0:T(8,128)(2,1)} %get-tuple-element.58.enc_hbm, f32[1,1024]{1,0:T(1,128)} %bitcast.32, ...), custom_call_target="tpu_custom_call" | custom-call | tf_op jit(solution)/shard_map/cond/branch_0_fun/gather_codes_29/pallas_call | solution.py:438
  59.6 0.0 copy-done
  59.7 0.0 copy-done.4
  59.7 7.8 %gradient_29.1 = (f32[640,1024]{1,0:T(8,128)}, f32[4,1024,1024]{2,1,0:T(8,128)}) custom-call(s32[32]{0:T(128)S(1)} %copy-done.4, bf16[4,464,1024]{2,1,0:T(8,128)(2,1)S(1)} %get-tuple-element.63.codes_ref, bf16[464,1024]{1,0:T(8,128)(2,1)S(1)} %get-tuple-element.64.residual_ref, bf16[464,1024]{1,0:T(8,128)(2,1)S(1)} %get-tuple-element.65.summed_ref, ...), custom_call_target="tpu_custom_call" | custom-call | tf_op jit(solution)/shard_map/cond/branch_0_fun/gradient_29/pallas_call | solution.py:489
Async XLA Ops:
  4.1 55.5 %copy-start = (f32[1024]{0:T(1024)S(1)}, f32[1024]{0:T(1024)}, u32[]{:S(2)}) copy-start(f32[1024]{0:T(1024)} %get-tuple-element.61) | copy-start | bytes 12292 | tf_op jit(solution)/shard_map/cond
  4.1 55.5 %copy-start.4 = (s32[32]{0:T(128)S(1)}, s32[32]{0:T(128)}, u32[]{:S(2)}) copy-start(s32[32]{0:T(128)} %get-tuple-element.56.live_hbm.live_ref) | copy-start | bytes 388 | tf_op jit(solution)/shard_map/cond
